TPU v7x, 32 devices: a whole 2x2x4 slice. The times are simulated.
32 devices in a mesh: seq: 8 (over z, x), chan: 4 (over y, core).
Axes of the slice: x: 2, y: 2, z: 4, core: 2. Of those that a mesh axis runs over, the one named last changes fastest.
Arguments:
- tokens: bfloat16 [2048, 8192], P('seq', 'chan'), may hold values from -700 to 700
- cotangent: bfloat16 [2048, 8192], P('seq', 'chan'), may hold values from -6 to 6
- filters: bfloat16 [256, 8192], P(None, 'chan'), may hold values from -0.375 to 0.375
- gain: float32 [8192], P('chan'), may hold values from 0.25 to 1.75
Outputs:
- conv_out: bfloat16 [2048, 8192], P('seq', 'chan')
- input_grad: bfloat16 [2048, 8192], P('seq', 'chan')
- filter_grad: float32 [256, 8192], P(None, 'chan')
- gain_grad: float32 [8192], P('chan')
All inputs are finite; a program needn't handle non-finite values.
Results may differ from a plain program's by a relative error of at most 0.005.
Values may be sent and summed in bfloat16 or wider, within the bound.
A program may use at most 64 MiB of HBM per device.

v0:
```python
import math

import jax
import jax.numpy as jnp
from jax import lax
from jax.sharding import PartitionSpec as P


def passed_along(block, axis, distance):
    devices = range(lax.axis_size(axis))
    route = [(i - distance, i) for i in devices if i - distance in devices]
    return lax.ppermute(block, axis, route)


def lag_conv(window, kernel, padding):
    channels = window.shape[1]
    result = lax.conv_general_dilated(
        window[None],
        kernel[:, None, :],
        (1,),
        (padding,),
        dimension_numbers=("NWC", "WIO", "NWC"),
        feature_group_count=channels,
        preferred_element_type=jnp.float32,
    )
    return result[0]


def local(tokens, cotangent, filters, gain):
    block_rows = tokens.shape[0]
    values = tokens.astype(jnp.float32)
    squares = lax.psum(jnp.sum(values * values, axis=1), "chan")
    model_width = gain.shape[0] * lax.axis_size("chan")
    factor = lax.rsqrt(squares / model_width + 1e-06)[:, None]
    normed = (values * factor * gain).astype(jnp.bfloat16)
    earlier = passed_along(normed, "seq", 1)
    window = jnp.concatenate([earlier, normed], axis=0)
    conv_out = lag_conv(window[1:], filters[::-1], (0, 0)).astype(jnp.bfloat16)
    local_part = lag_conv(cotangent, filters, (0, block_rows - 1))
    carried = lag_conv(cotangent[: block_rows - 1], filters[1:], (block_rows - 1, 0))
    upstream = local_part + passed_along(carried, "seq", -1)
    all_tokens = block_rows * lax.axis_size("seq")
    norm_factor = 1.0 / math.sqrt(all_tokens)
    lagged = lag_conv(window, cotangent, (0, 0))
    filter_terms = lagged[1:][::-1] * norm_factor
    gain_terms = jnp.sum(upstream * values * factor, axis=0) * norm_factor
    filter_grad, gain_grad = lax.psum((filter_terms, gain_terms), "seq")
    return (conv_out, upstream.astype(jnp.bfloat16), filter_grad, gain_grad)


def solution(mesh):
    placed = (P("seq", "chan"), P("seq", "chan"), P(None, "chan"), P("chan"))
    return jax.shard_map(
        local,
        mesh=mesh,
        in_specs=placed,
        out_specs=(P("seq", "chan"), P("seq", "chan"), P(None, "chan"), P("chan")),
        check_vma=False,
    )
```

profile of v0, /device:TPU:26, one launch (start us, length us, event | category | flops | bytes accessed | tf_op | source)
XLA Modules:
  0.0 352.3 jit_solution(6502999006746182411)
XLA Ops:
  7.2 0.0 all-reduce.2.cloned.1.call-start
  7.2 1.8 slice_bitcast_fusion
  9.0 52.6 %fusion.20 = f32[1,256,2048]{2,0,1:T(1,128)S(1)} fusion(bf16[255,1,2048]{2,0,1:T(8,128)(2,1)S(1)} %get-tuple-element.7, bf16[1,255,2048]{2,1,0:T(8,128)(2,1)S(1)} %get-tuple-element.8), kind=kOutput, calls=%fused_computation.27 | convolution fusion | flops 133693440 | bytes 4186112 | tf_op jit(solution)/shard_map/conv_general_dilated | solution.py:17
  61.7 0.0 copy-start
  61.7 0.0 copy-start.1
  61.7 0.0 copy-start.5
  61.7 2.2 copy.52
  63.9 3.8 %collective-permute-start.1 = (f32[256,2048]{1,0:T(8,128)}, f32[256,2048]{1,0:T(8,128)}, u32[]{:S(2)}, u32[]{:S(2)}) collective-permute-start(f32[256,2048]{1,0:T(8,128)} %bitcast.25), channel_id=1, source_target_pairs={{4,0},{8,4},{12,8},{16,12},{20,16},{24,20},{28,24},{5,1},{9,5},{13... | collective-permute-start | bytes 6291464 | tf_op jit(solution)/shard_map/ppermute | solution.py:12
  67.7 0.0 copy-done
  67.7 0.3 fusion.10
  68.0 6.3 %psum.21 = f32[256]{0:T(256)S(1)} all-reduce(f32[256]{0:T(256)S(1)} %fusion.10), channel_id=1, replica_groups=mesh['seq'=8,'chan'=4] {'chan'}, use_global_device_ids=true, to_apply=%region_1.0 | all-reduce | flops 256 | bytes 2048 | tf_op jit(solution)/shard_map/psum | solution.py:32
  74.4 0.0 copy-done.1
  74.4 0.0 copy-done.5
  74.4 0.0 copy-start.7
  74.4 53.7 %fusion.16 = f32[1,256,2048]{2,0,1:T(1,128)S(1)} fusion(bf16[256,1,2048]{2,0,1:T(8,128)(2,1)S(1)} %bitcast.28, bf16[1,256,2048]{2,1,0:T(8,128)(2,1)S(1)} %bitcast.31), kind=kOutput, calls=%fused_computation.23 | convolution fusion | flops 134742016 | bytes 4194304 | tf_op jit(solution)/shard_map/conv_general_dilated | solution.py:17
  128.1 0.0 collective-permute-done.1
  128.1 0.0 copy-done.7
  128.1 3.9 %fusion.14 = (f32[2048]{0:T(1024)S(1)}, bf16[256,2048]{1,0:T(8,128)(2,1)}, bf16[256,2048]{1,0:T(8,128)(2,1)S(1)}) fusion(bf16[256,2048]{1,0:T(8,128)(2,1)S(1)} %copy-done, f32[256]{0:T(256)S(1)} %add_rsqrt_fusion, f32[256,2048]{1,0:T(8,128)} %collective-permute-done.1, f32[1,256,2048]{2,0,1:T(1,128)S(1)} %fusion.16, f32[2048]{0:T(1024)S(1)} %copy-done.7), kind=kLoop, calls=%fused_computation.18 | loop fusion | flops 4716544 | bytes 7357440 | tf_op jit(solution)/shard_map/reduce_sum | solution.py:46
  132.0 1.3 collective-permute-start
  133.3 10.3 %rev.6 = bf16[256,2048]{1,0:T(8,128)(2,1)} reverse(bf16[256,2048]{1,0:T(8,128)(2,1)S(1)} %copy-done.1), dimensions={0} | reverse | bytes 2097152 | tf_op jit(solution)/shard_map/rev | solution.py:38
  143.6 25.2 %psum.23 = f32[2048]{0:T(1024)} all-reduce(f32[2048]{0:T(1024)S(1)} %broadcast_multiply_fusion.1), channel_id=1, replica_groups=mesh['seq'=8,'chan'=4] {'seq'}, use_global_device_ids=true, to_apply=%region_4.0 | all-reduce | flops 2048 | bytes 16384 | tf_op jit(solution)/shard_map/psum | solution.py:47
  168.8 0.0 copy-start.6
  168.8 0.0 collective-permute-done
  168.8 0.0 copy-start.2
  168.8 0.1 fusion.9
  168.9 0.8 copy-done.2
  169.8 0.6 copy-done.6
  170.4 55.1 %fusion = f32[1,256,2048]{2,0,1:T(1,128)S(1)} fusion(bf16[1,512,2048]{2,1,0:T(8,128)(2,1)S(1)} %fusion.9, bf16[256,1,2048]{2,0,1:T(8,128)(2,1)S(1)} %bitcast.32), kind=kOutput, calls=%fused_computation | convolution fusion | flops 268435456 | bytes 5242880 | tf_op jit(solution)/shard_map/slice | solution.py:45
  225.5 0.9 copy.51
  226.3 10.3 %rev.7 = f32[256,2048]{1,0:T(8,128)} reverse(f32[256,2048]{1,0:T(8,128)S(1)} %bitcast.27), dimensions={0} | reverse | bytes 4194304 | tf_op jit(solution)/shard_map/rev | solution.py:45
  236.7 3.2 broadcast_multiply_fusion
  239.9 0.0 copy-start.3
  239.9 0.0 all-reduce.2.cloned.1.call-update
  239.9 1.2 copy-done.3
  241.1 0.0 copy-start.4
  241.1 0.5 fusion.8
  241.6 0.7 copy-done.4
  242.3 54.1 %fusion.4 = bf16[1,256,2048]{2,0,1:T(2,128)(2,1)S(1)} fusion(bf16[1,511,2048]{2,1,0:T(8,128)(2,1)S(1)} %fusion.8, bf16[256,1,2048]{2,0,1:T(8,128)(2,1)S(1)} %bitcast.30), kind=kOutput, calls=%fused_computation.7 | convolution fusion | flops 268959744 | bytes 4190208 | tf_op jit(solution)/shard_map/conv_general_dilated | solution.py:17
  296.5 1.6 copy.53
  298.0 44.3 %all-reduce.2.cloned.1.call-done = f32[256,2048]{1,0:T(8,128)} async-done(((f32[256,2048]{1,0:T(8,128)}), f32[256,2048]{1,0:T(8,128)}) %all-reduce.2.cloned.1.call-update) | async-done | bytes 2097168 | tf_op jit(solution)/shard_map/psum | solution.py:47
  342.3 3.1 copy.55
  (2 shorter events, 0.0 us)
Async XLA Ops:
  7.2 335.1 %all-reduce.2.cloned.1.call-start = ((), (), s32[]{:S(2)}) async-start(), calls=%async_computation | async-start | bytes 4194304 | tf_op jit(solution)/shard_map/psum | solution.py:47
  61.7 6.0 %copy-start = (bf16[256,2048]{1,0:T(8,128)(2,1)S(1)}, bf16[256,2048]{1,0:T(8,128)(2,1)}, u32[]{:S(2)}) copy-start(bf16[256,2048]{1,0:T(8,128)(2,1)} %param.4) | copy-start | bytes 3145732
  61.7 12.7 %copy-start.1 = (bf16[256,2048]{1,0:T(8,128)(2,1)S(1)}, bf16[256,2048]{1,0:T(8,128)(2,1)}, u32[]{:S(2)}) copy-start(bf16[256,2048]{1,0:T(8,128)(2,1)} %param.6) | copy-start | bytes 3145732
  61.7 12.6 %copy-start.5 = (bf16[256,2048]{1,0:T(8,128)(2,1)S(1)}, bf16[256,2048]{1,0:T(8,128)(2,1)}, u32[]{:S(2)}) copy-start(bf16[256,2048]{1,0:T(8,128)(2,1)} %param.5) | copy-start | bytes 3145732
  63.9 64.1 %collective-permute-start.1 = (f32[256,2048]{1,0:T(8,128)}, f32[256,2048]{1,0:T(8,128)}, u32[]{:S(2)}, u32[]{:S(2)}) collective-permute-start(f32[256,2048]{1,0:T(8,128)} %bitcast.25), channel_id=1, source_target_pairs={{4,0},{8,4},{12,8},{16,12},{20,16},{24,20},{28,24},{5,1},{9,5},{13... | collective-permute-start | bytes 6291464 | tf_op jit(solution)/shard_map/ppermute | solution.py:12
  74.4 53.7 %copy-start.7 = (f32[2048]{0:T(1024)S(1)}, f32[2048]{0:T(1024)}, u32[]{:S(2)}) copy-start(f32[2048]{0:T(1024)} %param.7) | copy-start | bytes 24580
  132.0 36.8 %collective-permute-start = (bf16[256,2048]{1,0:T(8,128)(2,1)S(1)}, bf16[256,2048]{1,0:T(8,128)(2,1)S(1)}, u32[]{:S(2)}, u32[]{:S(2)}) collective-permute-start(bf16[256,2048]{1,0:T(8,128)(2,1)S(1)} %get-tuple-element.6), channel_id=1, source_target_pairs={{0,4},{4,8},{8,12},{12,16},{16,20},{20,24},{24,28},{1,5},{5,9},{9,... | collective-permute-start | bytes 3145736 | tf_op jit(solution)/shard_map/ppermute | solution.py:12
  168.8 1.6 copy-start.6
  168.8 1.0 copy-start.2
  239.9 1.2 copy-start.3
  241.1 1.2 copy-start.4
Sparse Core Ops, SparseCore 0:
  240.0 102.2 all-reduce.1
where the time goes:
time: 356 us; the launch traced here: 352 us
  matrix products  216 us (61%)
  waiting for transfers between devices  44.3 us (12%)
  local copies, waits for them, and re-layouts  33.6 us (9%)
  blocking collectives  31.5 us (9%)
  between operations  14.2 us (4%)
  other arithmetic  8.04 us (2%)
  starting transfers between devices  5.1 us (1%)
    conv_general_dilated x3, matrix products, lag_conv(): lax.conv_general_dilated(window[None], kernel[:, None, :], (1,), (padding...  160 us
    slice x1, matrix products, local(): filter_terms = lagged[1:][::-1] * norm_factor  55.1 us
    psum x1, waiting for transfers between devices, local(): filter_grad, gain_grad = lax.psum((filter_terms, gain_terms), 'seq')  44.3 us
    psum x1, blocking collectives, local(): filter_grad, gain_grad = lax.psum((filter_terms, gain_terms), 'seq')  25.2 us
    unnamed x20, local copies, waits for them, and re-layouts  11.2 us
    rev x1, local copies, waits for them, and re-layouts, local(): filter_terms = lagged[1:][::-1] * norm_factor  10.3 us
    rev x1, local copies, waits for them, and re-layouts, local(): conv_out = lag_conv(window[1:], filters[::-1], (0, 0)).astype(jnp.bfloat16)  10.3 us
  transfers between devices with their start and end apart: 3, of which 1 were waited for; matrix products, arithmetic and copies ran while one was open for 34% of the time, Pallas kernels for 0%

commit v1 on v0

v1 whole, which is shorter than its diff:
```python
import functools
import math

import jax
import jax.numpy as jnp
import ml_dtypes
import numpy as np
from jax import lax
from jax.experimental import pallas as pl
from jax.experimental.pallas import tpu as pltpu
from jax.sharding import PartitionSpec as P

MESH = pl.DeviceIdType.MESH


def halves(matrix):
    high = matrix.astype(ml_dtypes.bfloat16)
    low = (matrix - high.astype(np.float64)).astype(ml_dtypes.bfloat16)
    return high, low


def transforms(rows):
    odd = 2 * np.arange(rows)[:, None] + 1
    angle = np.pi / (2 * rows) * ((odd * np.arange(rows)[None, :]) % (4 * rows))
    forward = np.concatenate([np.cos(angle), -np.sin(angle)], axis=0)
    return (*halves(forward), *halves(forward.T / rows))


def kernel(
    sizes,
    tok, cot, fil, gain, fh, fl, ih, il,
    conv, igrad, fgrad, ggrad,
    htok, hcot, hfac, ssq, fac, spec_h, spec_a, spec_g, part, rs, ag, gsum,
    tok_s, tok_r, cot_s, cot_r, fac_s, fac_r, ssq_s, ssq_r, rs_s, rs_r, ag_s, ag_r, gs_s, gs_r,
):
    shards, groups, chunks, width, piece, owners, model_width, scale = sizes
    rows = tok.shape[0]
    me, my_chan = lax.axis_index("seq"), lax.axis_index("chan")
    nxt, prv = lax.rem(me + 1, shards), lax.rem(me + shards - 1, shards)
    sign = (1 - 2 * (lax.broadcasted_iota(jnp.int32, (rows, width), 0) & 1)).astype(jnp.float32)

    def cols(k):
        return pl.ds(pl.multiple_of(k * width, width), width)

    def every(count, body):
        lax.fori_loop(0, count, lambda i, c: (body(i), c)[1], 0)

    def others(count, mine, body):
        def step(i):
            @pl.when(i != mine)
            def _():
                body(i)
        every(count, step)

    def remote(src, dst, ssem, rsem, seq, chan):
        return pltpu.make_async_remote_copy(
            src_ref=src, dst_ref=dst, send_sem=ssem, recv_sem=rsem, device_id=(seq, chan), device_id_type=MESH)

    def cot_copy(k):
        return remote(cot.at[:, cols(k)], hcot.at[k], cot_s.at[k], cot_r.at[k], prv, my_chan)

    def tok_copy(k):
        return remote(tok.at[:, cols(k)], htok.at[k], tok_s.at[k], tok_r.at[k], nxt, my_chan)

    def fac_copy():
        return remote(fac, hfac, fac_s, fac_r, nxt, my_chan)

    def ssq_copy(to, at):
        return remote(ssq.at[at], ssq.at[at], ssq_s.at[to], ssq_r.at[at], me, to)

    def owned(o):
        return pl.ds(pl.multiple_of(o * piece, piece), piece)

    def rs_copy(k, to, at):
        return remote(part.at[k, owned(to)], rs.at[k, at], rs_s.at[k, to], rs_r.at[k, at], to, my_chan)

    def ag_copy(k, to, at):
        return remote(ag.at[k, owned(at)], ag.at[k, owned(at)], ag_s.at[k, to], ag_r.at[k, at], to, my_chan)

    def gs_copy(to, at):
        return remote(gsum.at[at], gsum.at[at], gs_s.at[to], gs_r.at[at], to, my_chan)

    def forward(x):
        return (jnp.dot(fh[...], x, preferred_element_type=jnp.float32)
                + jnp.dot(fl[...], x, preferred_element_type=jnp.float32))

    def inverse(real, imag):
        both = jnp.concatenate([real, imag], axis=0)
        high = both.astype(jnp.bfloat16)
        low = (both - high.astype(jnp.float32)).astype(jnp.bfloat16)
        return (jnp.dot(ih[...], high, preferred_element_type=jnp.float32)
                + jnp.dot(ih[...], low, preferred_element_type=jnp.float32)
                + jnp.dot(il[...], high, preferred_element_type=jnp.float32))

    def column(row):
        return jnp.transpose(jnp.broadcast_to(row, (128, rows)))[:, 0:1]

    barrier = pltpu.get_barrier_semaphore()
    others(shards, me, lambda p: pl.semaphore_signal(barrier, inc=1, device_id=(p, my_chan), device_id_type=MESH))
    others(groups, my_chan, lambda p: pl.semaphore_signal(barrier, inc=1, device_id=(me, p), device_id_type=MESH))
    pl.semaphore_wait(barrier, shards + groups - 2)

    @pl.when(me > 0)
    def _():
        every(chunks, lambda k: cot_copy(k).start())

    @pl.when(me < shards - 1)
    def _():
        every(chunks, lambda k: tok_copy(k).start())

    @pl.when(me == 0)
    def _():
        htok[...] = jnp.zeros_like(htok)
        hfac[...] = jnp.zeros_like(hfac)

    @pl.when(me == shards - 1)
    def _():
        hcot[...] = jnp.zeros_like(hcot)

    def squares(k, total):
        v = tok[:, cols(k)].astype(jnp.float32)
        return total + jnp.sum(v * v, axis=1, keepdims=True)

    total = lax.fori_loop(0, chunks, squares, jnp.zeros((rows, 1), jnp.float32))
    ssq[my_chan] = jnp.transpose(jnp.broadcast_to(total, (rows, 128)))[0:8]
    others(groups, my_chan, lambda p: ssq_copy(p, my_chan).start())

    def first(k):
        spec_h[k] = forward(fil[:, cols(k)])
        spec_g[k] = forward(cot[:, cols(k)])

    every(chunks, first)
    others(groups, my_chan, lambda p: ssq_copy(my_chan, p).wait_recv())
    fac[...] = lax.rsqrt(jnp.sum(ssq[...], axis=0) / model_width + 1e-06)

    @pl.when(me < shards - 1)
    def _():
        fac_copy().start()

    own_fac = column(fac[0:1])

    def second(k):
        at = cols(k)
        normed = (tok[:, at].astype(jnp.float32) * own_fac * gain[:, at]).astype(jnp.bfloat16)
        spec_a[k] = forward(normed)

    every(chunks, second)

    def backward(k):
        at = cols(k)

        @pl.when(me < shards - 1)
        def _():
            cot_copy(k).wait_recv()
        later = forward(hcot[k])
        g_r = spec_g[k, :rows] + sign * later[rows:]
        g_i = spec_g[k, rows:] - sign * later[:rows]
        a_r, a_i = spec_a[k, :rows], spec_a[k, rows:]
        terms = inverse(g_r * a_r + g_i * a_i, g_i * a_r - g_r * a_i) * scale
        part[k] = terms.astype(jnp.bfloat16)
        others(owners, me, lambda o: rs_copy(k, o, me).start())
        h_r, h_i = spec_h[k, :rows], spec_h[k, rows:]
        upstream = inverse(g_r * h_r + g_i * h_i, g_i * h_r - g_r * h_i)
        igrad[:, at] = upstream.astype(jnp.bfloat16)
        unit = tok[:, at].astype(jnp.float32) * own_fac
        gsum[me, :, at] = jnp.sum(upstream * unit, axis=0, keepdims=True) * scale

    every(chunks, backward)
    others(shards, me, lambda p: gs_copy(p, me).start())

    @pl.when(me > 0)
    def _():
        fac_copy().wait_recv()
    past_fac = column(hfac[0:1])

    def onward(k):
        at = cols(k)

        @pl.when(me > 0)
        def _():
            tok_copy(k).wait_recv()
        normed = (htok[k].astype(jnp.float32) * past_fac * gain[:, at]).astype(jnp.bfloat16)
        past = forward(normed)
        x_r = spec_a[k, :rows] - sign * past[rows:]
        x_i = spec_a[k, rows:] + sign * past[:rows]
        h_r, h_i = spec_h[k, :rows], spec_h[k, rows:]
        conv[:, at] = inverse(x_r * h_r - x_i * h_i, x_r * h_i + x_i * h_r).astype(jnp.bfloat16)

    def gather(k):
        @pl.when(me < owners)
        def _():
            others(shards, me, lambda p: rs_copy(k, me, p).wait_recv())
            rs[k, me] = part[k, owned(me)]
            summed = lax.fori_loop(
                0, shards, lambda p, acc: acc + rs[k, p].astype(jnp.float32), jnp.zeros((piece, width), jnp.float32))
            ag[k, owned(me)] = summed.astype(jnp.bfloat16)
            others(shards, me, lambda p: ag_copy(k, p, me).start())

    def both(k):
        gather(k)
        onward(k)

    every(chunks, both)
    others(shards, me, lambda p: gs_copy(me, p).wait_recv())
    ggrad[...] = jnp.sum(gsum[...], axis=0)

    def finish(k):
        others(owners, me, lambda o: ag_copy(k, me, o).wait_recv())
        fgrad[:, cols(k)] = ag[k].astype(jnp.float32)

    every(chunks, finish)

    others(groups, my_chan, lambda p: ssq_copy(p, my_chan).wait_send())
    others(shards, me, lambda p: gs_copy(p, me).wait_send())

    @pl.when(me > 0)
    def _():
        every(chunks, lambda k: cot_copy(k).wait_send())

    @pl.when(me < shards - 1)
    def _():
        every(chunks, lambda k: tok_copy(k).wait_send())
        fac_copy().wait_send()

    def drained(k):
        others(owners, me, lambda o: rs_copy(k, o, me).wait_send())

        @pl.when(me < owners)
        def _():
            others(shards, me, lambda p: ag_copy(k, p, me).wait_send())

    every(chunks, drained)


def local(tokens, cotangent, filters, gain):
    rows, channels = tokens.shape
    shards, groups = lax.axis_size("seq"), lax.axis_size("chan")
    width = 512 if channels % 512 == 0 else channels
    chunks = channels // width
    piece = max(16, rows // shards)
    owners = rows // piece
    sizes = (shards, groups, chunks, width, piece, owners, channels * groups, 1.0 / math.sqrt(rows * shards))
    vmem = pl.BlockSpec(memory_space=pltpu.VMEM)
    f32, bf16 = jnp.float32, jnp.bfloat16
    dma = pltpu.SemaphoreType.DMA
    conv, igrad, fgrad, ggrad = pl.pallas_call(
        functools.partial(kernel, sizes),
        out_shape=(
            jax.ShapeDtypeStruct((rows, channels), bf16),
            jax.ShapeDtypeStruct((rows, channels), bf16),
            jax.ShapeDtypeStruct((rows, channels), f32),
            jax.ShapeDtypeStruct((1, channels), f32),
        ),
        in_specs=[vmem] * 8,
        out_specs=(vmem,) * 4,
        scratch_shapes=[
            pltpu.VMEM((chunks, rows, width), bf16),
            pltpu.VMEM((chunks, rows, width), bf16),
            pltpu.VMEM((8, rows), f32),
            pltpu.VMEM((groups, 8, rows), f32),
            pltpu.VMEM((8, rows), f32),
            pltpu.VMEM((chunks, 2 * rows, width), f32),
            pltpu.VMEM((chunks, 2 * rows, width), f32),
            pltpu.VMEM((chunks, 2 * rows, width), f32),
            pltpu.VMEM((chunks, rows, width), bf16),
            pltpu.VMEM((chunks, shards, piece, width), bf16),
            pltpu.VMEM((chunks, rows, width), bf16),
            pltpu.VMEM((shards, 1, channels), f32),
            dma((chunks,)), dma((chunks,)), dma((chunks,)), dma((chunks,)),
            dma, dma,
            dma((groups,)), dma((groups,)),
            dma((chunks, owners)), dma((chunks, shards)),
            dma((chunks, shards)), dma((chunks, owners)),
            dma((shards,)), dma((shards,)),
        ],
        compiler_params=pltpu.CompilerParams(
            collective_id=0, has_side_effects=True, vmem_limit_bytes=56 * 1024 * 1024),
    )(tokens, cotangent, filters, gain[None], *(jnp.asarray(m) for m in transforms(rows)))
    return conv, igrad, fgrad, ggrad[0]


def solution(mesh):
    placed = (P("seq", "chan"), P("seq", "chan"), P(None, "chan"), P("chan"))
    return jax.shard_map(
        local,
        mesh=mesh,
        in_specs=placed,
        out_specs=(P("seq", "chan"), P("seq", "chan"), P(None, "chan"), P("chan")),
        check_vma=False,
    )
```

time: 356 us -> 106 us (0.30)
  the two profiles are of different devices: /device:TPU:26 before, /device:TPU:0 now
where the time goes in v1:
time: 106 us; the launch traced here: 105 us
  Pallas kernels  99.3 us (94%)
  local copies, waits for them, and re-layouts  5.36 us (5%)
    pallas_call x1, Pallas kernels, local(): pl.pallas_call(functools.partial(kernel, sizes), out_shape=(jax.ShapeDtyp...  99.3 us
    unnamed x10, local copies, waits for them, and re-layouts  5.36 us

profile of v1, /device:TPU:0, one launch (start us, length us, event | category | flops | bytes accessed | tf_op | source)
XLA Modules:
  0.0 105.4 jit_solution(1099835941328175988)
XLA Ops:
  0.6 99.3 %shard_map.111 = (bf16[256,2048]{1,0:T(8,128)(2,1)}, bf16[256,2048]{1,0:T(8,128)(2,1)}, f32[256,2048]{1,0:T(8,128)}, f32[1,2048]{1,0:T(1,128)}) custom-call(bf16[256,2048]{1,0:T(8,128)(2,1)} %tok.1, bf16[256,2048]{1,0:T(8,128)(2,1)} %cot.1, bf16[256,2048]{1,0:T(8,128)(2,1)} %fil.1, f32[1,2048]{1,0:T(1,128)} %bitcast.2, bf16[512,256]{1,0:T(8,128)(2,1)} %constant.8.clone.fh, ...), custom_call_target="tpu_custom_call" | custom-call | tf_op jit(solution)/shard_map/pallas_call | solution.py:246
  100.0 0.0 copy-start.1
  100.0 0.0 copy-start
  100.0 2.5 %copy.16 = bf16[256,2048]{1,0:T(8,128)(2,1)} copy(bf16[256,2048]{1,0:T(8,128)(2,1)} %get-tuple-element.16) | data formatting | bytes 2097152
  102.5 0.0 copy-done.1
  102.5 1.0 copy.17
  103.4 0.0 copy-done
  103.4 0.0 copy-start.2
  103.4 1.3 %copy.18 = f32[256,2048]{1,0:T(8,128)} copy(f32[256,2048]{1,0:T(8,128)S(1)} %copy-done) | data formatting | bytes 4194304
  104.7 0.0 copy-done.2
  104.8 0.6 copy.19
Async XLA Ops:
  100.0 2.5 %copy-start.1 = (bf16[256,2048]{1,0:T(8,128)(2,1)S(1)}, bf16[256,2048]{1,0:T(8,128)(2,1)}, u32[]{:S(2)}) copy-start(bf16[256,2048]{1,0:T(8,128)(2,1)} %get-tuple-element.17) | copy-start | bytes 3145732
  100.0 3.4 %copy-start = (f32[256,2048]{1,0:T(8,128)S(1)}, f32[256,2048]{1,0:T(8,128)}, u32[]{:S(2)}) copy-start(f32[256,2048]{1,0:T(8,128)} %get-tuple-element.18) | copy-start | bytes 6291460
  103.4 1.3 %copy-start.2 = (f32[1,2048]{1,0:T(1,128)S(1)}, f32[1,2048]{1,0:T(1,128)}, u32[]{:S(2)}) copy-start(f32[1,2048]{1,0:T(1,128)} %get-tuple-element.11) | copy-start | bytes 24580

commit v2 on v1

--- a/solution.py
+++ b/solution.py
@@ -30,12 +30,14 @@
     sizes,
     tok, cot, fil, gain, fh, fl, ih, il,
     conv, igrad, fgrad, ggrad,
-    htok, hcot, hfac, ssq, fac, spec_h, spec_a, spec_g, part, rs, ag, gsum,
-    tok_s, tok_r, cot_s, cot_r, fac_s, fac_r, ssq_s, ssq_r, rs_s, rs_r, ag_s, ag_r, gs_s, gs_r,
+    htok, hcot, hfac, ssq, fac, spec_h, spec_a, spec_g, part, rs, mine, near, ag, gsum,
+    tok_s, tok_r, cot_s, cot_r, fac_s, fac_r, ssq_s, ssq_r, near_s, near_r, rs_s, rs_r, ag_s, ag_r, gs_s, gs_r,
 ):
     shards, groups, chunks, width, piece, owners, model_width, scale = sizes
     rows = tok.shape[0]
     me, my_chan = lax.axis_index("seq"), lax.axis_index("chan")
+    pairs, side, spot = shards // 2, lax.rem(me, 2), lax.div(me, 2)
+    twin = me + 1 - 2 * side
     nxt, prv = lax.rem(me + 1, shards), lax.rem(me + shards - 1, shards)
     sign = (1 - 2 * (lax.broadcasted_iota(jnp.int32, (rows, width), 0) & 1)).astype(jnp.float32)
 
@@ -71,11 +73,15 @@
     def owned(o):
         return pl.ds(pl.multiple_of(o * piece, piece), piece)
 
+    def near_copy(k):
+        return remote(mine.at[k], near.at[k], near_s.at[k], near_r.at[k], twin, my_chan)
+
     def rs_copy(k, to, at):
-        return remote(part.at[k, owned(to)], rs.at[k, at], rs_s.at[k, to], rs_r.at[k, at], to, my_chan)
+        return remote(part.at[k, owned(to)], rs.at[k, at], rs_s.at[k, to], rs_r.at[k, at], 2 * to + side, my_chan)
 
     def ag_copy(k, to, at):
-        return remote(ag.at[k, owned(at)], ag.at[k, owned(at)], ag_s.at[k, to], ag_r.at[k, at], to, my_chan)
+        block = ag.at[k, owned(at)]
+        return remote(block, block, ag_s.at[k, to], ag_r.at[k, at], 2 * to + side, my_chan)
 
     def gs_copy(to, at):
         return remote(gsum.at[at], gsum.at[at], gs_s.at[to], gs_r.at[at], to, my_chan)
@@ -100,13 +106,17 @@
     others(groups, my_chan, lambda p: pl.semaphore_signal(barrier, inc=1, device_id=(me, p), device_id_type=MESH))
     pl.semaphore_wait(barrier, shards + groups - 2)
 
-    @pl.when(me > 0)
-    def _():
-        every(chunks, lambda k: cot_copy(k).start())
-
-    @pl.when(me < shards - 1)
-    def _():
-        every(chunks, lambda k: tok_copy(k).start())
+    def send_cot(k):
+        @pl.when(me > 0)
+        def _():
+            cot_copy(k).start()
+
+    def send_tok(k):
+        @pl.when(me < shards - 1)
+        def _():
+            tok_copy(k).start()
+
+    every(chunks, send_cot)
 
     @pl.when(me == 0)
     def _():
@@ -129,7 +139,7 @@
         spec_h[k] = forward(fil[:, cols(k)])
         spec_g[k] = forward(cot[:, cols(k)])
 
-    every(chunks, first)
+    first(0)
     others(groups, my_chan, lambda p: ssq_copy(my_chan, p).wait_recv())
     fac[...] = lax.rsqrt(jnp.sum(ssq[...], axis=0) / model_width + 1e-06)
 
@@ -143,8 +153,6 @@
         at = cols(k)
         normed = (tok[:, at].astype(jnp.float32) * own_fac * gain[:, at]).astype(jnp.bfloat16)
         spec_a[k] = forward(normed)
-
-    every(chunks, second)
 
     def backward(k):
         at = cols(k)
@@ -158,14 +166,31 @@
         a_r, a_i = spec_a[k, :rows], spec_a[k, rows:]
         terms = inverse(g_r * a_r + g_i * a_i, g_i * a_r - g_r * a_i) * scale
         part[k] = terms.astype(jnp.bfloat16)
-        others(owners, me, lambda o: rs_copy(k, o, me).start())
+        others(owners, spot, lambda o: rs_copy(k, o, spot).start())
         h_r, h_i = spec_h[k, :rows], spec_h[k, rows:]
         upstream = inverse(g_r * h_r + g_i * h_i, g_i * h_r - g_r * h_i)
         igrad[:, at] = upstream.astype(jnp.bfloat16)
         unit = tok[:, at].astype(jnp.float32) * own_fac
         gsum[me, :, at] = jnp.sum(upstream * unit, axis=0, keepdims=True) * scale
 
-    every(chunks, backward)
+    def reduce(k):
+        @pl.when(spot < owners)
+        def _():
+            others(pairs, spot, lambda p: rs_copy(k, spot, p).wait_recv())
+            rs[k, spot] = part[k, owned(spot)]
+            summed = lax.fori_loop(
+                0, pairs, lambda p, acc: acc + rs[k, p].astype(jnp.float32), jnp.zeros((piece, width), jnp.float32))
+            mine[k] = summed.astype(jnp.bfloat16)
+            near_copy(k).start()
+
+    for k in range(chunks):
+        if k > 0:
+            first(k)
+        second(k)
+        backward(k)
+        send_tok(k)
+        if k > 1:
+            reduce(k - 2)
     others(shards, me, lambda p: gs_copy(p, me).start())
 
     @pl.when(me > 0)
@@ -187,26 +212,27 @@
         conv[:, at] = inverse(x_r * h_r - x_i * h_i, x_r * h_i + x_i * h_r).astype(jnp.bfloat16)
 
     def gather(k):
-        @pl.when(me < owners)
-        def _():
-            others(shards, me, lambda p: rs_copy(k, me, p).wait_recv())
-            rs[k, me] = part[k, owned(me)]
-            summed = lax.fori_loop(
-                0, shards, lambda p, acc: acc + rs[k, p].astype(jnp.float32), jnp.zeros((piece, width), jnp.float32))
-            ag[k, owned(me)] = summed.astype(jnp.bfloat16)
-            others(shards, me, lambda p: ag_copy(k, p, me).start())
-
-    def both(k):
-        gather(k)
+        @pl.when(spot < owners)
+        def _():
+            near_copy(k).wait_recv()
+            summed = mine[k].astype(jnp.float32) + near[k].astype(jnp.float32)
+            ag[k, owned(spot)] = summed.astype(jnp.bfloat16)
+            others(pairs, spot, lambda p: ag_copy(k, p, spot).start())
+
+    behind = [k - 2 for k in range(2, chunks)]
+    for k in range(chunks):
+        if k not in behind:
+            reduce(k)
+        if k > 0:
+            gather(k - 1)
         onward(k)
-
-    every(chunks, both)
+    gather(chunks - 1)
     others(shards, me, lambda p: gs_copy(me, p).wait_recv())
     ggrad[...] = jnp.sum(gsum[...], axis=0)
 
     def finish(k):
-        others(owners, me, lambda o: ag_copy(k, me, o).wait_recv())
-        fgrad[:, cols(k)] = ag[k].astype(jnp.float32)
+        others(owners, spot, lambda o: ag_copy(k, spot, o).wait_recv())
+        fgrad[:, cols(k)] = ag[k]
 
     every(chunks, finish)
 
@@ -223,11 +249,12 @@
         fac_copy().wait_send()
 
     def drained(k):
-        others(owners, me, lambda o: rs_copy(k, o, me).wait_send())
-
-        @pl.when(me < owners)
-        def _():
-            others(shards, me, lambda p: ag_copy(k, p, me).wait_send())
+        others(owners, spot, lambda o: rs_copy(k, o, spot).wait_send())
+
+        @pl.when(spot < owners)
+        def _():
+            near_copy(k).wait_send()
+            others(pairs, spot, lambda p: ag_copy(k, p, spot).wait_send())
 
     every(chunks, drained)
 
@@ -237,7 +264,8 @@
     shards, groups = lax.axis_size("seq"), lax.axis_size("chan")
     width = 512 if channels % 512 == 0 else channels
     chunks = channels // width
-    piece = max(16, rows // shards)
+    pairs = shards // 2
+    piece = max(16, rows // pairs)
     owners = rows // piece
     sizes = (shards, groups, chunks, width, piece, owners, channels * groups, 1.0 / math.sqrt(rows * shards))
     vmem = pl.BlockSpec(memory_space=pltpu.VMEM)
@@ -248,7 +276,7 @@
         out_shape=(
             jax.ShapeDtypeStruct((rows, channels), bf16),
             jax.ShapeDtypeStruct((rows, channels), bf16),
-            jax.ShapeDtypeStruct((rows, channels), f32),
+            jax.ShapeDtypeStruct((rows, channels), bf16),
             jax.ShapeDtypeStruct((1, channels), f32),
         ),
         in_specs=[vmem] * 8,
@@ -263,20 +291,23 @@
             pltpu.VMEM((chunks, 2 * rows, width), f32),
             pltpu.VMEM((chunks, 2 * rows, width), f32),
             pltpu.VMEM((chunks, rows, width), bf16),
-            pltpu.VMEM((chunks, shards, piece, width), bf16),
+            pltpu.VMEM((chunks, pairs, piece, width), bf16),
+            pltpu.VMEM((chunks, piece, width), bf16),
+            pltpu.VMEM((chunks, piece, width), bf16),
             pltpu.VMEM((chunks, rows, width), bf16),
             pltpu.VMEM((shards, 1, channels), f32),
             dma((chunks,)), dma((chunks,)), dma((chunks,)), dma((chunks,)),
             dma, dma,
             dma((groups,)), dma((groups,)),
-            dma((chunks, owners)), dma((chunks, shards)),
-            dma((chunks, shards)), dma((chunks, owners)),
+            dma((chunks,)), dma((chunks,)),
+            dma((chunks, owners)), dma((chunks, pairs)),
+            dma((chunks, pairs)), dma((chunks, owners)),
             dma((shards,)), dma((shards,)),
         ],
         compiler_params=pltpu.CompilerParams(
             collective_id=0, has_side_effects=True, vmem_limit_bytes=56 * 1024 * 1024),
     )(tokens, cotangent, filters, gain[None], *(jnp.asarray(m) for m in transforms(rows)))
-    return conv, igrad, fgrad, ggrad[0]
+    return conv, igrad, fgrad.astype(f32), ggrad[0]
 
 
 def solution(mesh):

time: 106 us -> 91.8 us (0.87)
  the two profiles are of different devices: /device:TPU:0 before, /device:TPU:26 now
where the time goes in v2:
time: 91.8 us; the launch traced here: 91.7 us
  Pallas kernels  85.5 us (93%)
  other arithmetic  2.94 us (3%)
  local copies, waits for them, and re-layouts  2.55 us (3%)
    pallas_call x1, Pallas kernels, local(): pl.pallas_call(functools.partial(kernel, sizes), out_shape=(jax.ShapeDtyp...  85.5 us
    convert_element_type x1, other arithmetic, local(): return (conv, igrad, fgrad.astype(f32), ggrad[0])  2.94 us
    unnamed x9, local copies, waits for them, and re-layouts  2.55 us

profile of v2, /device:TPU:26, one launch (start us, length us, event | category | flops | bytes accessed | tf_op | source)
XLA Modules:
  0.0 91.7 jit_solution(7538834525957593191)
XLA Ops:
  0.6 85.5 %shard_map.111 = (bf16[256,2048]{1,0:T(8,128)(2,1)}, bf16[256,2048]{1,0:T(8,128)(2,1)}, bf16[256,2048]{1,0:T(8,128)(2,1)}, f32[1,2048]{1,0:T(1,128)}) custom-call(bf16[256,2048]{1,0:T(8,128)(2,1)} %tok.1, bf16[256,2048]{1,0:T(8,128)(2,1)} %cot.1, bf16[256,2048]{1,0:T(8,128)(2,1)} %fil.1, f32[1,2048]{1,0:T(1,128)} %bitcast.2, ...), custom_call_target="tpu_custom_call" | custom-call | tf_op jit(solution)/shard_map/pallas_call | solution.py:274
  86.2 0.0 copy-start.1
  86.2 0.0 copy-start
  86.2 2.9 %convert_element_type.3 = f32[256,2048]{1,0:T(8,128)} convert(bf16[256,2048]{1,0:T(8,128)(2,1)} %get-tuple-element.10) | non-fusion elementwise | flops 524288 | bytes 3145728 | tf_op jit(solution)/shard_map/convert_element_type | solution.py:310
  89.1 0.0 copy-done.1
  89.1 0.0 copy-start.2
  89.1 1.0 %copy.15 = bf16[256,2048]{1,0:T(8,128)(2,1)} copy(bf16[256,2048]{1,0:T(8,128)(2,1)S(1)} %copy-done.1) | data formatting | bytes 2097152
  90.1 0.0 copy-done
  90.1 1.0 %copy.16 = bf16[256,2048]{1,0:T(8,128)(2,1)} copy(bf16[256,2048]{1,0:T(8,128)(2,1)S(1)} %copy-done) | data formatting | bytes 2097152
  91.1 0.0 copy-done.2
  91.1 0.6 copy.17
Async XLA Ops:
  86.2 3.0 %copy-start.1 = (bf16[256,2048]{1,0:T(8,128)(2,1)S(1)}, bf16[256,2048]{1,0:T(8,128)(2,1)}, u32[]{:S(2)}) copy-start(bf16[256,2048]{1,0:T(8,128)(2,1)} %get-tuple-element.16) | copy-start | bytes 3145732
  86.2 3.9 %copy-start = (bf16[256,2048]{1,0:T(8,128)(2,1)S(1)}, bf16[256,2048]{1,0:T(8,128)(2,1)}, u32[]{:S(2)}) copy-start(bf16[256,2048]{1,0:T(8,128)(2,1)} %get-tuple-element.17) | copy-start | bytes 3145732
  89.1 1.9 %copy-start.2 = (f32[1,2048]{1,0:T(1,128)S(1)}, f32[1,2048]{1,0:T(1,128)}, u32[]{:S(2)}) copy-start(f32[1,2048]{1,0:T(1,128)} %get-tuple-element.11) | copy-start | bytes 24580

commit v3 on v2

--- a/solution.py
+++ b/solution.py
@@ -262,7 +262,7 @@
 def local(tokens, cotangent, filters, gain):
     rows, channels = tokens.shape
     shards, groups = lax.axis_size("seq"), lax.axis_size("chan")
-    width = 512 if channels % 512 == 0 else channels
+    width = 256 if channels % 256 == 0 else channels
     chunks = channels // width
     pairs = shards // 2
     piece = max(16, rows // pairs)

time: 91.8 us -> 91.2 us (level)
  no operation moved by 1% of the time
where the time goes in v3:
time: 91.2 us; the launch traced here: 91 us
  Pallas kernels  84.9 us (93%)
  other arithmetic  2.94 us (3%)
  local copies, waits for them, and re-layouts  2.55 us (3%)
    pallas_call x1, Pallas kernels, local(): pl.pallas_call(functools.partial(kernel, sizes), out_shape=(jax.ShapeDtyp...  84.9 us
    convert_element_type x1, other arithmetic, local(): return (conv, igrad, fgrad.astype(f32), ggrad[0])  2.94 us
    unnamed x9, local copies, waits for them, and re-layouts  2.55 us

profile of v3, /device:TPU:26, one launch (start us, length us, event | category | flops | bytes accessed | tf_op | source)
XLA Modules:
  0.0 91.0 jit_solution(8482770293803336218)
XLA Ops:
  0.6 84.9 %shard_map.111 = (bf16[256,2048]{1,0:T(8,128)(2,1)}, bf16[256,2048]{1,0:T(8,128)(2,1)}, bf16[256,2048]{1,0:T(8,128)(2,1)}, f32[1,2048]{1,0:T(1,128)}) custom-call(bf16[256,2048]{1,0:T(8,128)(2,1)} %tok.1, bf16[256,2048]{1,0:T(8,128)(2,1)} %cot.1, bf16[256,2048]{1,0:T(8,128)(2,1)} %fil.1, f32[1,2048]{1,0:T(1,128)} %bitcast.2, ...), custom_call_target="tpu_custom_call" | custom-call | tf_op jit(solution)/shard_map/pallas_call | solution.py:274
  85.5 0.0 copy-start.1
  85.5 0.0 copy-start
  85.5 2.9 %convert_element_type.3 = f32[256,2048]{1,0:T(8,128)} convert(bf16[256,2048]{1,0:T(8,128)(2,1)} %get-tuple-element.10) | non-fusion elementwise | flops 524288 | bytes 3145728 | tf_op jit(solution)/shard_map/convert_element_type | solution.py:310
  88.5 0.0 copy-done.1
  88.5 0.0 copy-start.2
  88.5 1.0 %copy.15 = bf16[256,2048]{1,0:T(8,128)(2,1)} copy(bf16[256,2048]{1,0:T(8,128)(2,1)S(1)} %copy-done.1) | data formatting | bytes 2097152
  89.4 0.0 copy-done
  89.4 1.0 %copy.16 = bf16[256,2048]{1,0:T(8,128)(2,1)} copy(bf16[256,2048]{1,0:T(8,128)(2,1)S(1)} %copy-done) | data formatting | bytes 2097152
  90.4 0.0 copy-done.2
  90.4 0.6 copy.17
Async XLA Ops:
  85.5 3.0 %copy-start.1 = (bf16[256,2048]{1,0:T(8,128)(2,1)S(1)}, bf16[256,2048]{1,0:T(8,128)(2,1)}, u32[]{:S(2)}) copy-start(bf16[256,2048]{1,0:T(8,128)(2,1)} %get-tuple-element.16) | copy-start | bytes 3145732
  85.5 3.9 %copy-start = (bf16[256,2048]{1,0:T(8,128)(2,1)S(1)}, bf16[256,2048]{1,0:T(8,128)(2,1)}, u32[]{:S(2)}) copy-start(bf16[256,2048]{1,0:T(8,128)(2,1)} %get-tuple-element.17) | copy-start | bytes 3145732
  88.5 1.9 %copy-start.2 = (f32[1,2048]{1,0:T(1,128)S(1)}, f32[1,2048]{1,0:T(1,128)}, u32[]{:S(2)}) copy-start(f32[1,2048]{1,0:T(1,128)} %get-tuple-element.11) | copy-start | bytes 24580
